TPU v7x, 256 devices: a whole 4x4x8 slice. The times are simulated.
256 devices in a mesh: copy: 4 (over x_hi, core), space: 64 (over y, z, x_lo).
Axes of the slice: x: 4 (x_hi: 2, x_lo: 2; x = x_hi * 2 + x_lo), y: 4, z: 8, core: 2. Of those that a mesh axis runs over, the one named last changes fastest.
Arguments:
- noisy_tokens: bfloat16 [4, 256, 256, 384], P('copy', 'space'), may hold values from -6 to 6
- grad_out: bfloat16 [4, 256, 256, 384], P('copy', 'space'), may hold values from -6 to 6
- filter_weight: bfloat16 [2, 256, 256, 384], P(None, None, 'space'), may hold values from -4 to 4
- weight_in: bfloat16 [384, 1536], replicated, may hold values from -0.3125 to 0.3125
- weight_out: bfloat16 [1536, 384], replicated, may hold values from -0.15625 to 0.15625
- gain_one: float32 [384], replicated, may hold values from 0.1 to 1.9
- gain_two: float32 [384], replicated, may hold values from 0.1 to 1.9
Outputs:
- block_out: bfloat16 [4, 256, 256, 384], P('copy', 'space')
- grad_tokens: bfloat16 [4, 256, 256, 384], P('copy', 'space')
- grad_filter: float32 [2, 256, 256, 384], P(None, None, 'space')
- grad_weight_in: bfloat16 [384, 1536], replicated
- grad_weight_out: bfloat16 [1536, 384], replicated
- grad_gain_one: float32 [384], replicated
- grad_gain_two: float32 [384], replicated
All inputs are finite; a program needn't handle non-finite values.
Results may differ from a plain program's by a relative error of at most 0.024.
Values may be sent and summed in bfloat16 or wider, within the bound.
A program may use at most 128 MiB of HBM per device.

v0:
```python
import math

import jax
import jax.numpy as jnp
from jax import lax
from jax.sharding import PartitionSpec as P

EPS = 1e-06


def dft_parts(length):
    index = jnp.arange(length, dtype=jnp.int32)
    phase = index[:, None] * index[None, :] % length
    angle = phase.astype(jnp.float32) * (2.0 * math.pi / length)
    factor = 1.0 / math.sqrt(length)
    return (
        (jnp.cos(angle) * factor).astype(jnp.bfloat16),
        (jnp.sin(angle) * factor).astype(jnp.bfloat16),
    )


def row_table(length):
    cosine, sine = dft_parts(length)
    return jnp.stack([cosine, -sine])


def column_table(length, direction):
    cosine, sine = dft_parts(length)
    upper = jnp.stack([cosine, direction * sine], axis=1)
    lower = jnp.stack([-direction * sine, cosine], axis=1)
    return jnp.stack([upper, lower])


def layer_norm(values):
    centre = jnp.mean(values, axis=-1, keepdims=True)
    centred = values - centre
    variance = jnp.mean(centred * centred, axis=-1, keepdims=True)
    rstd_value = lax.rsqrt(variance + EPS)
    return (centred * rstd_value, rstd_value)


def norm_backward(upstream, normed, rstd_value, gain):
    scaled = upstream * gain
    result = (
        scaled
        - jnp.mean(scaled, axis=-1, keepdims=True)
        - normed * jnp.mean(scaled * normed, axis=-1, keepdims=True)
    ) * rstd_value
    lead = tuple(range(upstream.ndim - 1))
    return (result, jnp.sum(upstream * normed, axis=lead))


def apply_filter(spectrum, filter_weight, direction):
    real_part = spectrum[0].astype(jnp.float32)
    imag_part = spectrum[1].astype(jnp.float32)
    kernel_real = filter_weight[0].astype(jnp.float32)
    kernel_imag = direction * filter_weight[1].astype(jnp.float32)
    return jnp.stack(
        [
            kernel_real * real_part - kernel_imag * imag_part,
            kernel_real * imag_part + kernel_imag * real_part,
        ]
    )


def exact_gelu(values):
    return jax.nn.gelu(values, approximate=False)


def spectral(values, filter_weight, direction):
    width = values.shape[2]
    rows_tab = row_table(width)
    rows = jnp.einsum(
        "pkw,bhwc->pbhkc", rows_tab, values, preferred_element_type=jnp.float32
    ).astype(jnp.bfloat16)
    columns = lax.all_to_all(rows, "space", split_axis=3, concat_axis=2, tiled=True)
    height = columns.shape[2]
    spectrum = jnp.einsum(
        "qmph,pbhkc->qbmkc", column_table(height, 1), columns, preferred_element_type=jnp.float32
    ).astype(jnp.bfloat16)
    weighted = apply_filter(spectrum, filter_weight[:, None], direction).astype(jnp.bfloat16)
    returned = jnp.einsum(
        "qmph,pbhkc->qbmkc", column_table(height, -1), weighted, preferred_element_type=jnp.float32
    ).astype(jnp.bfloat16)
    back_rows = lax.all_to_all(returned, "space", split_axis=2, concat_axis=3, tiled=True)
    output = jnp.einsum("pkw,pbhkc->bhwc", rows_tab, back_rows, preferred_element_type=jnp.float32)
    return (output, spectrum)


def body(noisy_tokens, grad_out, filter_weight, weight_in, weight_out, gain_one, gain_two):
    batch, rows_dev, width, chans = noisy_tokens.shape
    inputs = noisy_tokens.astype(jnp.float32)
    normed_one, rstd_one = layer_norm(inputs)
    mixed_in = (normed_one * gain_one).astype(jnp.bfloat16)
    spatial, spectrum = spectral(mixed_in, filter_weight, 1)
    normed_two, rstd_two = layer_norm(spatial)
    mlp_in = (normed_two * gain_two).astype(jnp.bfloat16).reshape(-1, chans)
    preact = jnp.dot(mlp_in, weight_in, preferred_element_type=jnp.float32)
    activated = exact_gelu(preact).astype(jnp.bfloat16)
    mlp_out = jnp.dot(activated, weight_out, preferred_element_type=jnp.float32)
    block_out = (inputs + mlp_out.reshape(inputs.shape)).astype(jnp.bfloat16)
    upstream = grad_out.reshape(-1, chans)
    grad_act = jnp.dot(upstream, weight_out.T, preferred_element_type=jnp.float32)
    grad_pre = jax.vjp(exact_gelu, preact)[1](grad_act)[0].astype(jnp.bfloat16)
    sum_out = jnp.dot(activated.T, upstream, preferred_element_type=jnp.float32)
    sum_in = jnp.dot(mlp_in.T, grad_pre, preferred_element_type=jnp.float32)
    grad_mlp = jnp.dot(grad_pre, weight_in.T, preferred_element_type=jnp.float32).reshape(
        inputs.shape
    )
    grad_spatial, sum_gain_two = norm_backward(grad_mlp, normed_two, rstd_two, gain_two)
    back_spatial, adjoint = spectral(grad_spatial.astype(jnp.bfloat16), filter_weight, -1)
    spec_f = spectrum.astype(jnp.float32)
    adj_f = adjoint.astype(jnp.float32)
    filter_terms = jnp.stack(
        [
            jnp.sum(adj_f[0] * spec_f[0] + adj_f[1] * spec_f[1], axis=0),
            jnp.sum(adj_f[1] * spec_f[0] - adj_f[0] * spec_f[1], axis=0),
        ]
    )
    grad_filter = lax.psum(filter_terms.astype(jnp.bfloat16), "copy").astype(jnp.float32)
    grad_normed, sum_gain_one = norm_backward(back_spatial, normed_one, rstd_one, gain_one)
    grad_tokens = (grad_out.astype(jnp.float32) + grad_normed).astype(jnp.bfloat16)
    local_sums = (sum_in, sum_out, sum_gain_one, sum_gain_two)
    summed = lax.psum(
        (local_sums[0], local_sums[1], local_sums[2], local_sums[3]), ("copy", "space")
    )
    total_tokens = batch * lax.axis_size("copy") * rows_dev * lax.axis_size("space") * width
    factor = 1.0 / math.sqrt(total_tokens)
    return (
        block_out,
        grad_tokens,
        grad_filter,
        (summed[0] * factor).astype(jnp.bfloat16),
        (summed[1] * factor).astype(jnp.bfloat16),
        summed[2] * factor,
        summed[3] * factor,
    )


def solution(mesh):
    return jax.shard_map(
        body,
        mesh=mesh,
        in_specs=(
            P("copy", "space", None, None),
            P("copy", "space", None, None),
            P(None, None, "space", None),
            P(),
            P(),
            P(),
            P(),
        ),
        out_specs=(
            P("copy", "space", None, None),
            P("copy", "space", None, None),
            P(None, None, "space", None),
            P(),
            P(),
            P(),
            P(),
        ),
        check_vma=False,
    )
```

profile of v0, /device:TPU:2, one launch (start us, length us, event | category | flops | bytes accessed | tf_op | source)
XLA Modules:
  0.0 627.6 jit_solution(3767009619410764740)
XLA Ops:
  13.5 3.0 copy.69
  16.5 13.3 %all-to-all-start = ((bf16[2,1,4,256,384]{4,0,2,1,3:T(2,128)(2,1)}), bf16[2,1,4,256,384]{4,0,2,1,3:T(2,128)(2,1)}, u32[]{:S(2)}, u32[]{:S(2)}) async-start(bf16[2,1,4,256,384]{4,0,2,1,3:T(2,128)(2,1)} %copy.69), calls=%async_computation | async-start | bytes 3145728 | tf_op jit(solution)/shard_map/all_to_all | solution.py:76
  38.2 30.3 %all-to-all-done = bf16[2,1,4,256,384]{4,0,2,1,3:T(2,128)(2,1)} async-done(((bf16[2,1,4,256,384]{4,0,2,1,3:T(2,128)(2,1)}), bf16[2,1,4,256,384]{4,0,2,1,3:T(2,128)(2,1)}, u32[]{:S(2)}, u32[]{:S(2)}) %all-to-all-start) | async-done | bytes 1572896 | tf_op jit(solution)/shard_map/all_to_all | solution.py:76
  77.5 4.3 copy.77
  81.8 45.8 %all_to_all.60 = bf16[2,1,256,4,384]{4,0,3,1,2:T(2,128)(2,1)S(1)} all-to-all(bf16[2,1,256,4,384]{4,0,3,1,2:T(2,128)(2,1)S(1)} %copy.77), channel_id=1, replica_groups=mesh['copy'=4,'space'=64] {'space'}, dimensions={2} | all-to-all | bytes 3145728 | tf_op jit(solution)/shard_map/all_to_all | solution.py:85
  133.5 15.5 %multiply_convert_fusion = (bf16[1024,1536]{1,0:T(8,128)(2,1)}, f32[1024,1536]{1,0:T(8,128)S(1)}, f32[1024,1536]{1,0:T(8,128)S(1)}) fusion(bf16[1024,384]{1,0:T(8,128)(2,1)S(1)} %bitcast.255, bf16[384,1536]{1,0:T(8,128)(2,1)S(1)} %copy-done), kind=kOutput, calls=%fused_computation.3 | convolution fusion | flops 1310195712 | bytes 17694720 | tf_op jit(solution)/shard_map/dot_general | solution.py:98
  149.0 3.3 add_convert_fusion
  157.8 4.0 fusion.40
  161.8 4.9 copy.84
  166.7 7.3 %all-to-all-start.2 = ((bf16[2,1,4,256,384]{4,0,2,1,3:T(2,128)(2,1)}), bf16[2,1,4,256,384]{4,0,2,1,3:T(2,128)(2,1)S(1)}, u32[]{:S(2)}, u32[]{:S(2)}) async-start(bf16[2,1,4,256,384]{4,0,2,1,3:T(2,128)(2,1)} %copy.84), calls=%async_computation.2 | async-start | bytes 3145728 | tf_op jit(solution)/shard_map/all_to_all | solution.py:76
  174.3 5.2 fusion.98
  179.5 3.2 fusion.99
  182.7 32.3 %all-to-all-done.2 = bf16[2,1,4,256,384]{4,0,2,1,3:T(2,128)(2,1)S(1)} async-done(((bf16[2,1,4,256,384]{4,0,2,1,3:T(2,128)(2,1)}), bf16[2,1,4,256,384]{4,0,2,1,3:T(2,128)(2,1)S(1)}, u32[]{:S(2)}, u32[]{:S(2)}) %all-to-all-start.2) | async-done | bytes 1572896 | tf_op jit(solution)/shard_map/all_to_all | solution.py:76
  218.9 4.3 fusion.96
  225.3 3.1 copy.90
  228.4 7.8 %all-to-all-start.3 = ((bf16[2,1,256,4,384]{4,0,3,1,2:T(2,128)(2,1)}), bf16[2,1,256,4,384]{4,0,3,1,2:T(2,128)(2,1)S(1)}, u32[]{:S(2)}, u32[]{:S(2)}) async-start(bf16[2,1,256,4,384]{4,0,3,1,2:T(2,128)(2,1)} %copy.90), calls=%async_computation.3 | async-start | bytes 3145728 | tf_op jit(solution)/shard_map/all_to_all | solution.py:85
  236.5 3.4 fusion.57
  245.5 5.2 fusion.97
  250.7 3.0 copy.81
  253.7 215.0 %all-reduce.7.cloned.1.call-done = (f32[384,1536]{1,0:T(8,128)}, f32[1536,384]{1,0:T(8,128)}) async-done(((f32[384,1536]{1,0:T(8,128)}, f32[1536,384]{1,0:T(8,128)}), (f32[384,1536]{1,0:T(8,128)}, f32[1536,384]{1,0:T(8,128)})) %all-reduce.7.cloned.1.call-update) | async-done | bytes 4718608 | tf_op jit(solution)/shard_map/psum | solution.py:124
  472.9 52.6 %all-reduce.5.cloned.1.call-done = bf16[2,256,4,384]{1,3,2,0:T(8,128)(2,1)} async-done(((bf16[2,256,4,384]{1,3,2,0:T(8,128)(2,1)}), bf16[2,256,4,384]{1,3,2,0:T(8,128)(2,1)}) %all-reduce.5.cloned.1.call-update) | async-done | bytes 1572880 | tf_op jit(solution)/shard_map/psum | solution.py:120
  525.5 3.9 copy.100
  533.5 76.9 %all-reduce = (f32[384]{0:T(512)}, f32[384]{0:T(512)}) all-reduce(f32[384]{0:T(512)} %get-tuple-element.28, f32[384]{0:T(512)S(1)} %copy-done.27), channel_id=1, replica_groups=mesh['copy'=4,'space'=64] {'copy','space'}, use_global_device_ids=true, to_apply=%region_12.13 | all-reduce | flops 768 | bytes 6144 | tf_op jit(solution)/shard_map/psum | solution.py:124
  613.6 3.4 fusion.17
  (122 shorter events, 61.9 us)
Async XLA Ops:
  7.2 126.3 %copy-start = (bf16[384,1536]{1,0:T(8,128)(2,1)S(1)}, bf16[384,1536]{1,0:T(8,128)(2,1)}, u32[]{:S(2)}) copy-start(bf16[384,1536]{1,0:T(8,128)(2,1)} %param.10) | copy-start | bytes 3538948
  10.5 1.8 copy-start.28
  12.8 3.7 copy-start.25
  16.5 52.0 %all-to-all-start = ((bf16[2,1,4,256,384]{4,0,2,1,3:T(2,128)(2,1)}), bf16[2,1,4,256,384]{4,0,2,1,3:T(2,128)(2,1)}, u32[]{:S(2)}, u32[]{:S(2)}) async-start(bf16[2,1,4,256,384]{4,0,2,1,3:T(2,128)(2,1)} %copy.69), calls=%async_computation | async-start | bytes 3145728 | tf_op jit(solution)/shard_map/all_to_all | solution.py:76
  33.2 41.0 %copy-start.4 = (bf16[1,256,4,384]{1,3,2,0:T(8,128)(2,1)}, bf16[1,256,4,384]{1,3,2,0:T(8,128)(2,1)S(1)}, u32[]{:S(2)}) copy-start(bf16[1,256,4,384]{1,3,2,0:T(8,128)(2,1)S(1)} %copy.124) | copy-start | bytes 2359300
  35.1 39.2 %copy-start.6 = (bf16[1,256,4,384]{1,3,2,0:T(8,128)(2,1)}, bf16[1,256,4,384]{1,3,2,0:T(8,128)(2,1)S(1)}, u32[]{:S(2)}) copy-start(bf16[1,256,4,384]{1,3,2,0:T(8,128)(2,1)S(1)} %copy.126) | copy-start | bytes 2359300
  133.5 15.5 %copy-start.19 = (bf16[1,4,256,384]{3,2,1,0:T(8,128)(2,1)}, bf16[1,4,256,384]{3,2,1,0:T(8,128)(2,1)S(1)}, u32[]{:S(2)}) copy-start(bf16[1,4,256,384]{3,2,1,0:T(8,128)(2,1)S(1)} %multiply_convert_fusion.4) | copy-start | bytes 2359300
  133.5 15.5 %copy-start.17 = (bf16[1,4,256,384]{3,2,1,0:T(8,128)(2,1)S(1)}, bf16[1,4,256,384]{3,2,1,0:T(8,128)(2,1)}, u32[]{:S(2)}) copy-start(bf16[1,4,256,384]{3,2,1,0:T(8,128)(2,1)} %param.8) | copy-start | bytes 2359300
  133.5 15.5 %copy-start.30 = (bf16[1536,384]{1,0:T(8,128)(2,1)S(1)}, bf16[1536,384]{1,0:T(8,128)(2,1)}, u32[]{:S(2)}) copy-start(bf16[1536,384]{1,0:T(8,128)(2,1)} %param.11) | copy-start | bytes 3538948
  152.3 1.9 copy-start.31
  166.7 48.3 %all-to-all-start.2 = ((bf16[2,1,4,256,384]{4,0,2,1,3:T(2,128)(2,1)}), bf16[2,1,4,256,384]{4,0,2,1,3:T(2,128)(2,1)S(1)}, u32[]{:S(2)}, u32[]{:S(2)}) async-start(bf16[2,1,4,256,384]{4,0,2,1,3:T(2,128)(2,1)} %copy.84), calls=%async_computation.2 | async-start | bytes 3145728 | tf_op jit(solution)/shard_map/all_to_all | solution.py:76
  174.1 294.7 %all-reduce.7.cloned.1.call-start = ((), (), s32[]{:S(2)}) async-start(), calls=%async_computation.5 | async-start | bytes 9437184 | tf_op jit(solution)/shard_map/psum | solution.py:124
  174.3 5.2 copy-start.18
  174.3 5.2 copy-start.32
  218.9 4.3 copy-start.5
  218.9 4.3 copy-start.7
  228.4 301.0 %all-to-all-start.3 = ((bf16[2,1,256,4,384]{4,0,3,1,2:T(2,128)(2,1)}), bf16[2,1,256,4,384]{4,0,3,1,2:T(2,128)(2,1)S(1)}, u32[]{:S(2)}, u32[]{:S(2)}) async-start(bf16[2,1,256,4,384]{4,0,3,1,2:T(2,128)(2,1)} %copy.90), calls=%async_computation.3 | async-start | bytes 3145728 | tf_op jit(solution)/shard_map/all_to_all | solution.py:85
  236.2 289.3 %all-reduce.5.cloned.1.call-start = ((), (), s32[]{:S(2)}) async-start(), calls=%async_computation.4 | async-start | bytes 3145728 | tf_op jit(solution)/shard_map/psum | solution.py:120
  236.4 3.9 copy-start.1
  236.5 4.8 copy-start.2
  468.7 3.0 copy-start.10
  531.0 2.6 copy-start.27
  531.0 82.7 %copy-start.8 = (f32[1,4,256,384]{2,3,1,0:T(8,128)S(1)}, f32[1,4,256,384]{2,3,1,0:T(8,128)}, u32[]{:S(2)}) copy-start(f32[1,4,256,384]{2,3,1,0:T(8,128)} %copy.81) | copy-start | bytes 4718596
  617.1 2.4 copy-start.9
  (14 other events, 13.4 us)
Sparse Core Ops, SparseCore 0:
  182.9 285.8 all-reduce.6
  471.6 53.8 all-reduce.4
where the time goes:
time: 639 us; the launch traced here: 628 us
  waiting for transfers between devices  330 us (52%)
  blocking collectives  123 us (19%)
  matrix products  53.9 us (8%)
  local copies, waits for them, and re-layouts  50 us (8%)
  starting transfers between devices  28.9 us (5%)
  other arithmetic  27.3 us (4%)
  between operations  14.7 us (2%)
    psum x1, waiting for transfers between devices, body(): lax.psum((local_sums[0], local_sums[1], local_sums[2], local_sums[3]), ('...  215 us
    psum x1, blocking collectives, body(): lax.psum((local_sums[0], local_sums[1], local_sums[2], local_sums[3]), ('...  76.9 us
    all_to_all x2, waiting for transfers between devices, spectral(): lax.all_to_all(rows, 'space', split_axis=3, concat_axis=2, tiled=True)  62.6 us
    psum x1, waiting for transfers between devices, body(): lax.psum(filter_terms.astype(jnp.bfloat16), 'copy').astype(jnp.float32)  52.6 us
    all_to_all x1, blocking collectives, spectral(): lax.all_to_all(returned, 'space', split_axis=2, concat_axis=3, tiled=True)  45.8 us
    all_to_all x2, starting transfers between devices, spectral(): lax.all_to_all(rows, 'space', split_axis=3, concat_axis=2, tiled=True)  20.6 us
    unnamed x73, local copies, waits for them, and re-layouts  17.3 us
    dot_general x1, matrix products, body(): preact = jnp.dot(mlp_in, weight_in, preferred_element_type=jnp.float32)  15.5 us
  transfers between devices with their start and end apart: 5, of which 4 were waited for; matrix products, arithmetic and copies ran while one was open for 9% of the time, Pallas kernels for 0%

commit v1 on v0

--- a/solution.py
+++ b/solution.py
@@ -1,11 +1,87 @@
+import functools
 import math
 
 import jax
 import jax.numpy as jnp
 from jax import lax
+from jax.experimental import pallas as pl
+from jax.experimental.pallas import tpu as pltpu
 from jax.sharding import PartitionSpec as P
 
+MESH = pl.DeviceIdType.MESH
+
 EPS = 1e-06
+
+
+def _copy_sum_kernel(n, rows, x_ref, o_ref, slots, send_sem, recv_sem, local_sem):
+    me = lax.axis_index("copy")
+    sp = lax.axis_index("space")
+    barrier = pltpu.get_barrier_semaphore()
+    for d in range(1, n):
+        peer = lax.rem(me + d, n)
+        pl.semaphore_signal(barrier, inc=1, device_id=(peer, sp), device_id_type=MESH)
+    pl.semaphore_wait(barrier, n - 1)
+    local = pltpu.make_async_copy(x_ref, slots.at[me], local_sem)
+    local.start()
+    sends = []
+    for d in range(1, n):
+        peer = lax.rem(me + d, n)
+        c = pltpu.make_async_remote_copy(
+            src_ref=x_ref,
+            dst_ref=slots.at[me],
+            send_sem=send_sem.at[d - 1],
+            recv_sem=recv_sem.at[me],
+            device_id=(peer, sp),
+            device_id_type=MESH,
+        )
+        c.start()
+        sends.append(c)
+    for d in range(1, n):
+        src = lax.rem(me + n - d, n)
+        pltpu.make_async_remote_copy(
+            src_ref=x_ref,
+            dst_ref=slots.at[src],
+            send_sem=send_sem.at[d - 1],
+            recv_sem=recv_sem.at[src],
+            device_id=(src, sp),
+            device_id_type=MESH,
+        ).wait_recv()
+    local.wait()
+    for c in sends:
+        c.wait_send()
+    block = 64
+
+    def body(i, carry):
+        r = pl.ds(pl.multiple_of(i * block, block), block)
+        acc = slots[0, r, :].astype(jnp.float32)
+        for j in range(1, n):
+            acc = acc + slots[j, r, :].astype(jnp.float32)
+        o_ref[r, :] = acc
+        return carry
+
+    lax.fori_loop(0, rows // block, body, 0)
+
+
+def copy_sum(x, n):
+    rows, cols = x.shape
+    return pl.pallas_call(
+        functools.partial(_copy_sum_kernel, n, rows),
+        out_shape=jax.ShapeDtypeStruct((rows, cols), jnp.float32),
+        in_specs=[pl.BlockSpec(memory_space=pltpu.VMEM)],
+        out_specs=pl.BlockSpec(memory_space=pltpu.VMEM),
+        scratch_shapes=[
+            pltpu.VMEM((n, rows, cols), x.dtype),
+            pltpu.SemaphoreType.DMA((n - 1,)),
+            pltpu.SemaphoreType.DMA((n,)),
+            pltpu.SemaphoreType.DMA,
+        ],
+        compiler_params=pltpu.CompilerParams(
+            collective_id=1, has_side_effects=True, vmem_limit_bytes=48 * 1024 * 1024
+        ),
+        cost_estimate=pl.CostEstimate(
+            flops=n * rows * cols, transcendentals=0, bytes_accessed=(n + 2) * rows * cols * 2
+        ),
+    )(x)
 
 
 def dft_parts(length):
@@ -117,23 +193,27 @@
             jnp.sum(adj_f[1] * spec_f[0] - adj_f[0] * spec_f[1], axis=0),
         ]
     )
-    grad_filter = lax.psum(filter_terms.astype(jnp.bfloat16), "copy").astype(jnp.float32)
+    fshape = filter_terms.shape
+    grad_filter = copy_sum(
+        filter_terms.astype(jnp.bfloat16).reshape(fshape[0] * fshape[1], fshape[2] * fshape[3]),
+        lax.axis_size("copy"),
+    ).reshape(fshape)
     grad_normed, sum_gain_one = norm_backward(back_spatial, normed_one, rstd_one, gain_one)
     grad_tokens = (grad_out.astype(jnp.float32) + grad_normed).astype(jnp.bfloat16)
-    local_sums = (sum_in, sum_out, sum_gain_one, sum_gain_two)
-    summed = lax.psum(
-        (local_sums[0], local_sums[1], local_sums[2], local_sums[3]), ("copy", "space")
-    )
     total_tokens = batch * lax.axis_size("copy") * rows_dev * lax.axis_size("space") * width
     factor = 1.0 / math.sqrt(total_tokens)
+    both = ("copy", "space")
+    weight_sums = lax.psum((sum_in.astype(jnp.bfloat16), sum_out.astype(jnp.bfloat16)), both)
+    weight_sums = [(s.astype(jnp.float32) * factor).astype(jnp.bfloat16) for s in weight_sums]
+    gains = lax.psum(lax.psum(jnp.stack([sum_gain_one, sum_gain_two]), "copy"), "space")
     return (
         block_out,
         grad_tokens,
         grad_filter,
-        (summed[0] * factor).astype(jnp.bfloat16),
-        (summed[1] * factor).astype(jnp.bfloat16),
-        summed[2] * factor,
-        summed[3] * factor,
+        weight_sums[0],
+        weight_sums[1],
+        gains[0] * factor,
+        gains[1] * factor,
     )
 
 

time: 639 us -> 795 us (1.24)
  blocking collectives: 123 us -> 210 us
  Pallas kernels: 0 us -> 71.1 us
  waiting for transfers between devices: 330 us -> 322 us
    psum x1 -> x2, blocking collectives: 76.9 us -> 164 us  [the longest x1 154 us: body(): lax.psum(lax.psum(jnp.stack([sum_gain_one, sum_gain_two]), 'copy'), 'space')]
    pallas_call x0 -> x1, Pallas kernels: none -> 71.1 us  [copy_sum(): pl.pallas_call(functools.partial(_copy_sum_kernel, n, rows), out_shape=ja...]
    psum x2 -> x1, waiting for transfers between devices: 268 us -> 259 us  [body(): lax.psum((sum_in.astype(jnp.bfloat16), sum_out.astype(jnp.bfloat16)), both)]
    unnamed x73 -> x71, local copies, waits for them, and re-layouts: 17.3 us -> 15.9 us
  transfers between devices with their start and end apart: 5 -> 4, of which waited for: 4 -> 3; matrix products, arithmetic and copies ran while one was open for 9% -> 6% of each run, Pallas kernels for 0% -> 9%
where the time goes in v1:
time: 795 us; the launch traced here: 784 us
  waiting for transfers between devices  322 us (41%)
  blocking collectives  210 us (26%)
  Pallas kernels  71.1 us (9%)
  local copies, waits for them, and re-layouts  57.2 us (7%)
  matrix products  55 us (7%)
  starting transfers between devices  28.5 us (4%)
  other arithmetic  24.7 us (3%)
  between operations  14.7 us (2%)
    psum x1, waiting for transfers between devices, body(): lax.psum((sum_in.astype(jnp.bfloat16), sum_out.astype(jnp.bfloat16)), both)  259 us
    psum x1, blocking collectives, body(): lax.psum(lax.psum(jnp.stack([sum_gain_one, sum_gain_two]), 'copy'), 'space')  154 us
    pallas_call x1, Pallas kernels, copy_sum(): pl.pallas_call(functools.partial(_copy_sum_kernel, n, rows), out_shape=ja...  71.1 us
    all_to_all x2, waiting for transfers between devices, spectral(): lax.all_to_all(rows, 'space', split_axis=3, concat_axis=2, tiled=True)  63.4 us
    all_to_all x1, blocking collectives, spectral(): lax.all_to_all(returned, 'space', split_axis=2, concat_axis=3, tiled=True)  45.8 us
    all_to_all x2, starting transfers between devices, spectral(): lax.all_to_all(rows, 'space', split_axis=3, concat_axis=2, tiled=True)  20.9 us
  transfers between devices with their start and end apart: 4, of which 3 were waited for; matrix products, arithmetic and copies ran while one was open for 6% of the time, Pallas kernels for 9%

profile of v1, /device:TPU:2, one launch (start us, length us, event | category | flops | bytes accessed | tf_op | source)
XLA Modules:
  0.0 783.9 jit_solution(7106026650946472999)
XLA Ops:
  16.5 13.3 %all-to-all-start = ((bf16[2,1,4,256,384]{4,0,2,1,3:T(2,128)(2,1)}), bf16[2,1,4,256,384]{4,0,2,1,3:T(2,128)(2,1)}, u32[]{:S(2)}, u32[]{:S(2)}) async-start(bf16[2,1,4,256,384]{4,0,2,1,3:T(2,128)(2,1)} %copy.69), calls=%async_computation | async-start | bytes 3145728 | tf_op jit(solution)/shard_map/all_to_all | solution.py:152
  38.2 30.3 %all-to-all-done = bf16[2,1,4,256,384]{4,0,2,1,3:T(2,128)(2,1)} async-done(((bf16[2,1,4,256,384]{4,0,2,1,3:T(2,128)(2,1)}), bf16[2,1,4,256,384]{4,0,2,1,3:T(2,128)(2,1)}, u32[]{:S(2)}, u32[]{:S(2)}) %all-to-all-start) | async-done | bytes 1572896 | tf_op jit(solution)/shard_map/all_to_all | solution.py:152
  77.5 4.3 copy.77
  81.9 45.8 %all_to_all.60 = bf16[2,1,256,4,384]{4,0,3,1,2:T(2,128)(2,1)S(1)} all-to-all(bf16[2,1,256,4,384]{4,0,3,1,2:T(2,128)(2,1)S(1)} %copy.77), channel_id=1, replica_groups=mesh['copy'=4,'space'=64] {'space'}, dimensions={2} | all-to-all | bytes 3145728 | tf_op jit(solution)/shard_map/all_to_all | solution.py:161
  133.6 15.5 %multiply_convert_fusion = (bf16[1024,1536]{1,0:T(8,128)(2,1)}, f32[1024,1536]{1,0:T(8,128)S(1)}, f32[1024,1536]{1,0:T(8,128)S(1)}) fusion(bf16[1024,384]{1,0:T(8,128)(2,1)S(1)} %bitcast.260, bf16[384,1536]{1,0:T(8,128)(2,1)S(1)} %copy-done), kind=kOutput, calls=%fused_computation.3 | convolution fusion | flops 1310195712 | bytes 17694720 | tf_op jit(solution)/shard_map/dot_general | solution.py:174
  149.1 3.3 add_convert_fusion
  158.0 3.9 fusion.40
  161.8 5.0 copy.84
  166.8 7.6 all-to-all-start.2
  174.4 4.9 convolution_convert_fusion
  179.4 33.1 %all-to-all-done.2 = bf16[2,1,4,256,384]{4,0,2,1,3:T(2,128)(2,1)S(1)} async-done(((bf16[2,1,4,256,384]{4,0,2,1,3:T(2,128)(2,1)}), bf16[2,1,4,256,384]{4,0,2,1,3:T(2,128)(2,1)S(1)}, u32[]{:S(2)}, u32[]{:S(2)}) %all-to-all-start.2) | async-done | bytes 1572896 | tf_op jit(solution)/shard_map/all_to_all | solution.py:152
  216.3 4.4 fusion.98
  222.8 3.2 copy.90
  226.0 7.4 all-to-all-start.3
  233.6 4.6 convolution_convert_fusion.1
  240.5 5.2 fusion.99
  245.6 3.1 copy.81
  248.7 259.0 %all-reduce.3.cloned.1.call-done = (bf16[384,1536]{1,0:T(8,128)(2,1)}, bf16[1536,384]{1,0:T(8,128)(2,1)}) async-done(((bf16[384,1536]{1,0:T(8,128)(2,1)}, bf16[1536,384]{1,0:T(8,128)(2,1)}), (bf16[384,1536]{1,0:T(8,128)(2,1)}, bf16[1536,384]{1,0:T(8,128)(2,1)})) %all-reduce.3.cloned.1.call-update) | async-done | bytes 2359312 | tf_op jit(solution)/shard_map/psum | solution.py:206
  516.3 3.8 copy.98
  521.7 71.1 %shard_map.126 = f32[512,1536]{1,0:T(8,128)S(1)} custom-call(bf16[512,1536]{1,0:T(8,128)(2,1)S(1)} %bitcast.246), custom_call_target="tpu_custom_call" | custom-call | flops 3145728 | bytes 9437184 | tf_op jit(solution)/shard_map/pallas_call | solution.py:67
  594.5 4.8 reshape.579
  603.5 10.6 %psum.30 = f32[2,384]{1,0:T(2,128)S(1)} all-reduce(f32[2,384]{1,0:T(2,128)S(1)} %pad_maximum_fusion.8), channel_id=1, replica_groups=mesh['copy'=4,'space'=64] {'copy'}, use_global_device_ids=true, to_apply=%region_12.13 | all-reduce | flops 768 | bytes 6144 | tf_op jit(solution)/shard_map/psum | solution.py:208
  614.1 153.8 %psum.31 = f32[2,384]{1,0:T(2,128)S(1)} all-reduce(f32[2,384]{1,0:T(2,128)S(1)} %psum.30), channel_id=1, replica_groups=mesh['copy'=4,'space'=64] {'space'}, use_global_device_ids=true, to_apply=%region_13.14 | all-reduce | flops 768 | bytes 6144 | tf_op jit(solution)/shard_map/psum | solution.py:208
  769.9 3.4 fusion.17
  (123 shorter events, 68.0 us)
Async XLA Ops:
  7.2 126.4 %copy-start = (bf16[384,1536]{1,0:T(8,128)(2,1)S(1)}, bf16[384,1536]{1,0:T(8,128)(2,1)}, u32[]{:S(2)}) copy-start(bf16[384,1536]{1,0:T(8,128)(2,1)} %param.10) | copy-start | bytes 3538948
  10.5 1.8 copy-start.28
  12.8 3.7 copy-start.25
  16.5 52.0 %all-to-all-start = ((bf16[2,1,4,256,384]{4,0,2,1,3:T(2,128)(2,1)}), bf16[2,1,4,256,384]{4,0,2,1,3:T(2,128)(2,1)}, u32[]{:S(2)}, u32[]{:S(2)}) async-start(bf16[2,1,4,256,384]{4,0,2,1,3:T(2,128)(2,1)} %copy.69), calls=%async_computation | async-start | bytes 3145728 | tf_op jit(solution)/shard_map/all_to_all | solution.py:152
  33.2 41.0 %copy-start.5 = (bf16[1,256,4,384]{1,3,2,0:T(8,128)(2,1)}, bf16[1,256,4,384]{1,3,2,0:T(8,128)(2,1)S(1)}, u32[]{:S(2)}) copy-start(bf16[1,256,4,384]{1,3,2,0:T(8,128)(2,1)S(1)} %copy.124) | copy-start | bytes 2359300
  35.1 39.2 %copy-start.7 = (bf16[1,256,4,384]{1,3,2,0:T(8,128)(2,1)}, bf16[1,256,4,384]{1,3,2,0:T(8,128)(2,1)S(1)}, u32[]{:S(2)}) copy-start(bf16[1,256,4,384]{1,3,2,0:T(8,128)(2,1)S(1)} %copy.126) | copy-start | bytes 2359300
  74.3 1.0 copy-start.22
  133.5 15.5 %copy-start.19 = (bf16[1,4,256,384]{3,2,1,0:T(8,128)(2,1)}, bf16[1,4,256,384]{3,2,1,0:T(8,128)(2,1)S(1)}, u32[]{:S(2)}) copy-start(bf16[1,4,256,384]{3,2,1,0:T(8,128)(2,1)S(1)} %multiply_convert_fusion.4) | copy-start | bytes 2359300
  133.5 15.5 %copy-start.18 = (bf16[1,4,256,384]{3,2,1,0:T(8,128)(2,1)S(1)}, bf16[1,4,256,384]{3,2,1,0:T(8,128)(2,1)}, u32[]{:S(2)}) copy-start(bf16[1,4,256,384]{3,2,1,0:T(8,128)(2,1)} %param.8) | copy-start | bytes 2359300
  133.6 15.5 %copy-start.30 = (bf16[1536,384]{1,0:T(8,128)(2,1)S(1)}, bf16[1536,384]{1,0:T(8,128)(2,1)}, u32[]{:S(2)}) copy-start(bf16[1536,384]{1,0:T(8,128)(2,1)} %param.11) | copy-start | bytes 3538948
  152.4 1.9 copy-start.31
  154.3 1.3 copy-start.4
  166.8 45.7 %all-to-all-start.2 = ((bf16[2,1,4,256,384]{4,0,2,1,3:T(2,128)(2,1)}), bf16[2,1,4,256,384]{4,0,2,1,3:T(2,128)(2,1)S(1)}, u32[]{:S(2)}, u32[]{:S(2)}) async-start(bf16[2,1,4,256,384]{4,0,2,1,3:T(2,128)(2,1)} %copy.84), calls=%async_computation.2 | async-start | bytes 3145728 | tf_op jit(solution)/shard_map/all_to_all | solution.py:152
  216.3 4.4 copy-start.6
  216.3 4.4 copy-start.8
  226.0 373.4 %all-to-all-start.3 = ((bf16[2,1,256,4,384]{4,0,3,1,2:T(2,128)(2,1)}), bf16[2,1,256,4,384]{4,0,3,1,2:T(2,128)(2,1)S(1)}, u32[]{:S(2)}, u32[]{:S(2)}) async-start(bf16[2,1,256,4,384]{4,0,3,1,2:T(2,128)(2,1)} %copy.90), calls=%async_computation.3 | async-start | bytes 3145728 | tf_op jit(solution)/shard_map/all_to_all | solution.py:161
  233.3 274.4 %all-reduce.3.cloned.1.call-start = ((), (), s32[]{:S(2)}) async-start(), calls=%async_computation.4 | async-start | bytes 4718592 | tf_op jit(solution)/shard_map/psum | solution.py:206
  238.1 2.3 copy-start.27
  507.7 2.7 copy-start.13
  507.7 3.9 copy-start.2
  511.6 2.8 copy-start.3
  592.9 1.7 copy-start.1
  600.9 169.0 %copy-start.9 = (f32[1,4,256,384]{2,3,1,0:T(8,128)S(1)}, f32[1,4,256,384]{2,3,1,0:T(8,128)}, u32[]{:S(2)}) copy-start(f32[1,4,256,384]{2,3,1,0:T(8,128)} %copy.81) | copy-start | bytes 4718596
  773.3 2.4 copy-start.10
  (12 other events, 11.2 us)
Sparse Core Ops, SparseCore 0:
  240.3 267.3 all-reduce.2

commit v2 on v0

--- a/solution.py
+++ b/solution.py
@@ -1,11 +1,149 @@
+import functools
 import math
 
 import jax
 import jax.numpy as jnp
 from jax import lax
+from jax.experimental import pallas as pl
+from jax.experimental.pallas import tpu as pltpu
 from jax.sharding import PartitionSpec as P
 
+MESH = pl.DeviceIdType.MESH
+
 EPS = 1e-06
+
+
+def _partner(idx, bit):
+    step = 1 << bit
+    flip = 1 - 2 * ((idx // step) % 2)
+    return idx + flip * step
+
+
+def _tree_sum_kernel(n_copy, n_space, x_ref, o_ref, send_buf, recv_buf, send_sem, recv_sem):
+    me_c = lax.axis_index("copy")
+    me_s = lax.axis_index("space")
+    bits = []
+    for b in range(n_space.bit_length() - 1):
+        bits.append(("space", b))
+    for b in range(n_copy.bit_length() - 1):
+        bits.append(("copy", b))
+
+    def peer(axis, b):
+        if axis == "space":
+            return (me_c, _partner(me_s, b))
+        return (_partner(me_c, b), me_s)
+
+    barrier = pltpu.get_barrier_semaphore()
+    for axis, b in bits:
+        pl.semaphore_signal(barrier, inc=1, device_id=peer(axis, b), device_id_type=MESH)
+    pl.semaphore_wait(barrier, len(bits))
+    acc = x_ref[...]
+    copies = []
+    for s, (axis, b) in enumerate(bits):
+        send_buf[s] = acc
+        c = pltpu.make_async_remote_copy(
+            src_ref=send_buf.at[s],
+            dst_ref=recv_buf.at[s],
+            send_sem=send_sem.at[s],
+            recv_sem=recv_sem.at[s],
+            device_id=peer(axis, b),
+            device_id_type=MESH,
+        )
+        c.start()
+        c.wait_recv()
+        copies.append(c)
+        acc = acc + recv_buf[s]
+    for c in copies:
+        c.wait_send()
+    o_ref[...] = acc
+
+
+def tree_sum(x, n_copy, n_space):
+    steps = (n_copy.bit_length() - 1) + (n_space.bit_length() - 1)
+    return pl.pallas_call(
+        functools.partial(_tree_sum_kernel, n_copy, n_space),
+        out_shape=jax.ShapeDtypeStruct(x.shape, jnp.float32),
+        in_specs=[pl.BlockSpec(memory_space=pltpu.VMEM)],
+        out_specs=pl.BlockSpec(memory_space=pltpu.VMEM),
+        scratch_shapes=[
+            pltpu.VMEM((steps,) + x.shape, jnp.float32),
+            pltpu.VMEM((steps,) + x.shape, jnp.float32),
+            pltpu.SemaphoreType.DMA((steps,)),
+            pltpu.SemaphoreType.DMA((steps,)),
+        ],
+        compiler_params=pltpu.CompilerParams(collective_id=2, has_side_effects=True),
+        cost_estimate=pl.CostEstimate(
+            flops=steps * x.size, transcendentals=0, bytes_accessed=4 * steps * x.size
+        ),
+    )(x)
+
+
+def _filter_sum_kernel(rows, x_ref, o_ref, half_in, part, other, full_in, sems):
+    me_c = lax.axis_index("copy")
+    me_s = lax.axis_index("space")
+    core = me_c % 2
+    hi = me_c // 2
+    mate = (me_c + 1 - 2 * core, me_s)
+    far = (me_c + 2 - 4 * hi, me_s)
+    half = rows // 2
+    barrier = pltpu.get_barrier_semaphore()
+    pl.semaphore_signal(barrier, inc=1, device_id=mate, device_id_type=MESH)
+    pl.semaphore_signal(barrier, inc=1, device_id=far, device_id_type=MESH)
+    pl.semaphore_wait(barrier, 2)
+    mine = pl.ds(pl.multiple_of(core * half, 8), half)
+    theirs = pl.ds(pl.multiple_of((1 - core) * half, 8), half)
+    c1 = pltpu.make_async_remote_copy(
+        src_ref=x_ref.at[theirs], dst_ref=half_in, send_sem=sems.at[0], recv_sem=sems.at[1],
+        device_id=mate, device_id_type=MESH)
+    c1.start()
+    c1.wait_recv()
+    own = x_ref[mine, :].astype(jnp.float32)
+    got = half_in[...].astype(jnp.float32)
+    first = jnp.where(core == 0, own, got)
+    second = jnp.where(core == 0, got, own)
+    part[...] = (first + second).astype(jnp.bfloat16)
+    c2 = pltpu.make_async_remote_copy(
+        src_ref=part, dst_ref=other, send_sem=sems.at[2], recv_sem=sems.at[3],
+        device_id=far, device_id_type=MESH)
+    c2.start()
+    c2.wait_recv()
+    mine_p = part[...].astype(jnp.float32)
+    got_p = other[...].astype(jnp.float32)
+    total = jnp.where(hi == 0, mine_p + got_p, got_p + mine_p)
+    o_ref[mine, :] = total
+    c3 = pltpu.make_async_remote_copy(
+        src_ref=o_ref.at[mine], dst_ref=full_in, send_sem=sems.at[4], recv_sem=sems.at[5],
+        device_id=mate, device_id_type=MESH)
+    c3.start()
+    c3.wait_recv()
+    o_ref[theirs, :] = full_in[...]
+    c1.wait_send()
+    c2.wait_send()
+    c3.wait_send()
+
+
+def filter_sum(x):
+    rows, cols = x.shape
+    half = rows // 2
+    return pl.pallas_call(
+        functools.partial(_filter_sum_kernel, rows),
+        out_shape=jax.ShapeDtypeStruct((rows, cols), jnp.float32),
+        in_specs=[pl.BlockSpec(memory_space=pltpu.VMEM)],
+        out_specs=pl.BlockSpec(memory_space=pltpu.VMEM),
+        scratch_shapes=[
+            pltpu.VMEM((half, cols), x.dtype),
+            pltpu.VMEM((half, cols), jnp.bfloat16),
+            pltpu.VMEM((half, cols), jnp.bfloat16),
+            pltpu.VMEM((half, cols), jnp.float32),
+            pltpu.SemaphoreType.DMA((6,)),
+        ],
+        compiler_params=pltpu.CompilerParams(
+            collective_id=1, has_side_effects=True, vmem_limit_bytes=48 * 1024 * 1024
+        ),
+        cost_estimate=pl.CostEstimate(
+            flops=2 * rows * cols, transcendentals=0, bytes_accessed=10 * rows * cols
+        ),
+    )(x)
 
 
 def dft_parts(length):
@@ -117,23 +255,28 @@
             jnp.sum(adj_f[1] * spec_f[0] - adj_f[0] * spec_f[1], axis=0),
         ]
     )
-    grad_filter = lax.psum(filter_terms.astype(jnp.bfloat16), "copy").astype(jnp.float32)
+    fshape = filter_terms.shape
+    grad_filter = filter_sum(
+        filter_terms.astype(jnp.bfloat16).reshape(fshape[0] * fshape[1], fshape[2] * fshape[3])
+    ).reshape(fshape)
     grad_normed, sum_gain_one = norm_backward(back_spatial, normed_one, rstd_one, gain_one)
     grad_tokens = (grad_out.astype(jnp.float32) + grad_normed).astype(jnp.bfloat16)
-    local_sums = (sum_in, sum_out, sum_gain_one, sum_gain_two)
-    summed = lax.psum(
-        (local_sums[0], local_sums[1], local_sums[2], local_sums[3]), ("copy", "space")
-    )
     total_tokens = batch * lax.axis_size("copy") * rows_dev * lax.axis_size("space") * width
     factor = 1.0 / math.sqrt(total_tokens)
+    both = ("copy", "space")
+    weight_sums = lax.psum((sum_in.astype(jnp.bfloat16), sum_out.astype(jnp.bfloat16)), both)
+    weight_sums = [(s.astype(jnp.float32) * factor).astype(jnp.bfloat16) for s in weight_sums]
+    gains = tree_sum(
+        jnp.stack([sum_gain_one, sum_gain_two]), lax.axis_size("copy"), lax.axis_size("space")
+    )
     return (
         block_out,
         grad_tokens,
         grad_filter,
-        (summed[0] * factor).astype(jnp.bfloat16),
-        (summed[1] * factor).astype(jnp.bfloat16),
-        summed[2] * factor,
-        summed[3] * factor,
+        weight_sums[0],
+        weight_sums[1],
+        gains[0] * factor,
+        gains[1] * factor,
     )
 
 

time: 639 us -> 615 us (0.962)
  blocking collectives: 123 us -> 45.8 us
  Pallas kernels: 0 us -> 54.3 us
  waiting for transfers between devices: 330 us -> 322 us
  local copies, waits for them, and re-layouts: 50 us -> 57.3 us
    psum x1 -> x0, blocking collectives: 76.9 us -> none  [body(): lax.psum((local_sums[0], local_sums[1], local_sums[2], local_sums[3]), ('...]
    pallas_call x0 -> x2, Pallas kernels: none -> 54.3 us  [the longest x1 28 us: tree_sum(): pl.pallas_call(functools.partial(_tree_sum_kernel, n_copy, n_space), out_...]
    psum x2 -> x1, waiting for transfers between devices: 268 us -> 259 us  [body(): lax.psum((sum_in.astype(jnp.bfloat16), sum_out.astype(jnp.bfloat16)), both)]
    unnamed x73 -> x71, local copies, waits for them, and re-layouts: 17.3 us -> 15.8 us
  transfers between devices with their start and end apart: 5 -> 4, of which waited for: 4 -> 3; matrix products, arithmetic and copies ran while one was open for 9% -> 7% of each run, Pallas kernels for 0% -> 4%
where the time goes in v2:
time: 615 us; the launch traced here: 603 us
  waiting for transfers between devices  322 us (52%)
  local copies, waits for them, and re-layouts  57.3 us (9%)
  matrix products  55 us (9%)
  Pallas kernels  54.3 us (9%)
  blocking collectives  45.8 us (7%)
  starting transfers between devices  28.5 us (5%)
  other arithmetic  25.4 us (4%)
  between operations  14.7 us (2%)
    psum x1, waiting for transfers between devices, body(): lax.psum((sum_in.astype(jnp.bfloat16), sum_out.astype(jnp.bfloat16)), both)  259 us
    all_to_all x2, waiting for transfers between devices, spectral(): lax.all_to_all(rows, 'space', split_axis=3, concat_axis=2, tiled=True)  63.4 us
    all_to_all x1, blocking collectives, spectral(): lax.all_to_all(returned, 'space', split_axis=2, concat_axis=3, tiled=True)  45.8 us
    pallas_call x1, Pallas kernels, tree_sum(): pl.pallas_call(functools.partial(_tree_sum_kernel, n_copy, n_space), out_...  28 us
    pallas_call x1, Pallas kernels, filter_sum(): pl.pallas_call(functools.partial(_filter_sum_kernel, rows), out_shape=jax...  26.2 us
    all_to_all x2, starting transfers between devices, spectral(): lax.all_to_all(rows, 'space', split_axis=3, concat_axis=2, tiled=True)  20.9 us
    unnamed x71, local copies, waits for them, and re-layouts  15.8 us
    dot_general x1, matrix products, body(): preact = jnp.dot(mlp_in, weight_in, preferred_element_type=jnp.float32)  15.5 us
  transfers between devices with their start and end apart: 4, of which 3 were waited for; matrix products, arithmetic and copies ran while one was open for 7% of the time, Pallas kernels for 4%

profile of v2, /device:TPU:2, one launch (start us, length us, event | category | flops | bytes accessed | tf_op | source)
XLA Modules:
  0.0 603.5 jit_solution(11377496529280471920)
XLA Ops:
  13.5 3.0 copy.69
  16.5 13.3 %all-to-all-start = ((bf16[2,1,4,256,384]{4,0,2,1,3:T(2,128)(2,1)}), bf16[2,1,4,256,384]{4,0,2,1,3:T(2,128)(2,1)}, u32[]{:S(2)}, u32[]{:S(2)}) async-start(bf16[2,1,4,256,384]{4,0,2,1,3:T(2,128)(2,1)} %copy.69), calls=%async_computation | async-start | bytes 3145728 | tf_op jit(solution)/shard_map/all_to_all | solution.py:214
  38.2 30.3 %all-to-all-done = bf16[2,1,4,256,384]{4,0,2,1,3:T(2,128)(2,1)} async-done(((bf16[2,1,4,256,384]{4,0,2,1,3:T(2,128)(2,1)}), bf16[2,1,4,256,384]{4,0,2,1,3:T(2,128)(2,1)}, u32[]{:S(2)}, u32[]{:S(2)}) %all-to-all-start) | async-done | bytes 1572896 | tf_op jit(solution)/shard_map/all_to_all | solution.py:214
  77.5 4.3 copy.77
  81.9 45.8 %all_to_all.60 = bf16[2,1,256,4,384]{4,0,3,1,2:T(2,128)(2,1)S(1)} all-to-all(bf16[2,1,256,4,384]{4,0,3,1,2:T(2,128)(2,1)S(1)} %copy.77), channel_id=1, replica_groups=mesh['copy'=4,'space'=64] {'space'}, dimensions={2} | all-to-all | bytes 3145728 | tf_op jit(solution)/shard_map/all_to_all | solution.py:223
  133.6 15.5 %multiply_convert_fusion = (bf16[1024,1536]{1,0:T(8,128)(2,1)}, f32[1024,1536]{1,0:T(8,128)S(1)}, f32[1024,1536]{1,0:T(8,128)S(1)}) fusion(bf16[1024,384]{1,0:T(8,128)(2,1)S(1)} %bitcast.260, bf16[384,1536]{1,0:T(8,128)(2,1)S(1)} %copy-done), kind=kOutput, calls=%fused_computation.3 | convolution fusion | flops 1310195712 | bytes 17694720 | tf_op jit(solution)/shard_map/dot_general | solution.py:236
  149.1 3.3 add_convert_fusion
  158.0 3.9 fusion.40
  161.8 5.0 copy.84
  166.8 7.6 %all-to-all-start.2 = ((bf16[2,1,4,256,384]{4,0,2,1,3:T(2,128)(2,1)}), bf16[2,1,4,256,384]{4,0,2,1,3:T(2,128)(2,1)S(1)}, u32[]{:S(2)}, u32[]{:S(2)}) async-start(bf16[2,1,4,256,384]{4,0,2,1,3:T(2,128)(2,1)} %copy.84), calls=%async_computation.2 | async-start | bytes 3145728 | tf_op jit(solution)/shard_map/all_to_all | solution.py:214
  174.4 4.9 convolution_convert_fusion
  179.4 33.1 %all-to-all-done.2 = bf16[2,1,4,256,384]{4,0,2,1,3:T(2,128)(2,1)S(1)} async-done(((bf16[2,1,4,256,384]{4,0,2,1,3:T(2,128)(2,1)}), bf16[2,1,4,256,384]{4,0,2,1,3:T(2,128)(2,1)S(1)}, u32[]{:S(2)}, u32[]{:S(2)}) %all-to-all-start.2) | async-done | bytes 1572896 | tf_op jit(solution)/shard_map/all_to_all | solution.py:214
  216.3 4.4 fusion.96
  222.7 3.2 copy.90
  225.9 7.4 %all-to-all-start.3 = ((bf16[2,1,256,4,384]{4,0,3,1,2:T(2,128)(2,1)}), bf16[2,1,256,4,384]{4,0,3,1,2:T(2,128)(2,1)S(1)}, u32[]{:S(2)}, u32[]{:S(2)}) async-start(bf16[2,1,256,4,384]{4,0,3,1,2:T(2,128)(2,1)} %copy.90), calls=%async_computation.3 | async-start | bytes 3145728 | tf_op jit(solution)/shard_map/all_to_all | solution.py:223
  233.5 4.6 convolution_convert_fusion.1
  240.4 5.2 fusion.97
  245.6 3.1 copy.81
  248.7 259.1 %all-reduce.3.cloned.1.call-done = (bf16[384,1536]{1,0:T(8,128)(2,1)}, bf16[1536,384]{1,0:T(8,128)(2,1)}) async-done(((bf16[384,1536]{1,0:T(8,128)(2,1)}, bf16[1536,384]{1,0:T(8,128)(2,1)}), (bf16[384,1536]{1,0:T(8,128)(2,1)}, bf16[1536,384]{1,0:T(8,128)(2,1)})) %all-reduce.3.cloned.1.call-update) | async-done | bytes 2359312 | tf_op jit(solution)/shard_map/psum | solution.py:267
  516.3 3.8 copy.98
  521.8 26.2 %shard_map.126 = f32[512,1536]{1,0:T(8,128)S(1)} custom-call(bf16[512,1536]{1,0:T(8,128)(2,1)S(1)} %bitcast.246), custom_call_target="tpu_custom_call" | custom-call | flops 1572864 | bytes 7864320 | tf_op jit(solution)/shard_map/pallas_call | solution.py:128
  554.5 4.9 reshape.579
  559.4 28.0 %shard_map.127 = f32[2,384]{1,0:T(2,128)} custom-call(f32[2,384]{1,0:T(2,128)} %pad_maximum_fusion.8.x_ref), custom_call_target="tpu_custom_call" | custom-call | flops 6144 | bytes 24576 | tf_op jit(solution)/shard_map/pallas_call | solution.py:63
  589.5 3.4 fusion.17
  (122 shorter events, 65.6 us)
Async XLA Ops:
  7.2 126.4 %copy-start = (bf16[384,1536]{1,0:T(8,128)(2,1)S(1)}, bf16[384,1536]{1,0:T(8,128)(2,1)}, u32[]{:S(2)}) copy-start(bf16[384,1536]{1,0:T(8,128)(2,1)} %param.10) | copy-start | bytes 3538948
  10.5 1.8 copy-start.28
  12.9 3.7 copy-start.25
  16.5 52.0 %all-to-all-start = ((bf16[2,1,4,256,384]{4,0,2,1,3:T(2,128)(2,1)}), bf16[2,1,4,256,384]{4,0,2,1,3:T(2,128)(2,1)}, u32[]{:S(2)}, u32[]{:S(2)}) async-start(bf16[2,1,4,256,384]{4,0,2,1,3:T(2,128)(2,1)} %copy.69), calls=%async_computation | async-start | bytes 3145728 | tf_op jit(solution)/shard_map/all_to_all | solution.py:214
  33.3 41.0 %copy-start.5 = (bf16[1,256,4,384]{1,3,2,0:T(8,128)(2,1)}, bf16[1,256,4,384]{1,3,2,0:T(8,128)(2,1)S(1)}, u32[]{:S(2)}) copy-start(bf16[1,256,4,384]{1,3,2,0:T(8,128)(2,1)S(1)} %copy.124) | copy-start | bytes 2359300
  35.1 39.2 %copy-start.7 = (bf16[1,256,4,384]{1,3,2,0:T(8,128)(2,1)}, bf16[1,256,4,384]{1,3,2,0:T(8,128)(2,1)S(1)}, u32[]{:S(2)}) copy-start(bf16[1,256,4,384]{1,3,2,0:T(8,128)(2,1)S(1)} %copy.126) | copy-start | bytes 2359300
  74.3 1.0 copy-start.22
  133.5 15.5 %copy-start.19 = (bf16[1,4,256,384]{3,2,1,0:T(8,128)(2,1)}, bf16[1,4,256,384]{3,2,1,0:T(8,128)(2,1)S(1)}, u32[]{:S(2)}) copy-start(bf16[1,4,256,384]{3,2,1,0:T(8,128)(2,1)S(1)} %multiply_convert_fusion.4) | copy-start | bytes 2359300
  133.5 15.5 %copy-start.18 = (bf16[1,4,256,384]{3,2,1,0:T(8,128)(2,1)S(1)}, bf16[1,4,256,384]{3,2,1,0:T(8,128)(2,1)}, u32[]{:S(2)}) copy-start(bf16[1,4,256,384]{3,2,1,0:T(8,128)(2,1)} %param.8) | copy-start | bytes 2359300
  133.5 15.5 %copy-start.30 = (bf16[1536,384]{1,0:T(8,128)(2,1)S(1)}, bf16[1536,384]{1,0:T(8,128)(2,1)}, u32[]{:S(2)}) copy-start(bf16[1536,384]{1,0:T(8,128)(2,1)} %param.11) | copy-start | bytes 3538948
  152.4 1.9 copy-start.31
  154.3 1.2 copy-start.4
  166.8 45.7 %all-to-all-start.2 = ((bf16[2,1,4,256,384]{4,0,2,1,3:T(2,128)(2,1)}), bf16[2,1,4,256,384]{4,0,2,1,3:T(2,128)(2,1)S(1)}, u32[]{:S(2)}, u32[]{:S(2)}) async-start(bf16[2,1,4,256,384]{4,0,2,1,3:T(2,128)(2,1)} %copy.84), calls=%async_computation.2 | async-start | bytes 3145728 | tf_op jit(solution)/shard_map/all_to_all | solution.py:214
  216.3 4.4 copy-start.6
  216.3 4.4 copy-start.8
  225.9 323.8 %all-to-all-start.3 = ((bf16[2,1,256,4,384]{4,0,3,1,2:T(2,128)(2,1)}), bf16[2,1,256,4,384]{4,0,3,1,2:T(2,128)(2,1)S(1)}, u32[]{:S(2)}, u32[]{:S(2)}) async-start(bf16[2,1,256,4,384]{4,0,3,1,2:T(2,128)(2,1)} %copy.90), calls=%async_computation.3 | async-start | bytes 3145728 | tf_op jit(solution)/shard_map/all_to_all | solution.py:223
  233.3 274.5 %all-reduce.3.cloned.1.call-start = ((), (), s32[]{:S(2)}) async-start(), calls=%async_computation.4 | async-start | bytes 4718592 | tf_op jit(solution)/shard_map/psum | solution.py:267
  238.1 2.3 copy-start.27
  507.7 2.7 copy-start.13
  507.7 3.9 copy-start.2
  511.6 2.8 copy-start.3
  548.0 1.7 copy-start.1
  554.5 35.0 %copy-start.9 = (f32[1,4,256,384]{2,3,1,0:T(8,128)S(1)}, f32[1,4,256,384]{2,3,1,0:T(8,128)}, u32[]{:S(2)}) copy-start(f32[1,4,256,384]{2,3,1,0:T(8,128)} %copy.81) | copy-start | bytes 4718596
  592.9 2.4 copy-start.10
  (12 other events, 11.2 us)
Sparse Core Ops, SparseCore 0:
  240.3 267.3 all-reduce.2
